TPU v7x, 128 devices: a whole 4x4x4 slice. The times are simulated.
128 devices in a mesh: ctx: 8 (over x, z_lo), head: 16 (over z_hi, y, core).
Axes of the slice: x: 4, y: 4, z: 4 (z_hi: 2, z_lo: 2; z = z_hi * 2 + z_lo), core: 2. Of those that a mesh axis runs over, the one named last changes fastest.
Arguments:
- queries: bfloat16 [256, 16384], P(None, 'head'), may hold values from -64 to 64, as said below
- grad_out: bfloat16 [256, 16384], P(None, 'head'), may hold values from -24 to 24
- latent: bfloat16 [16384, 512], P(('ctx', 'head')), may hold values from -6.1 to 6.1
- up_key: bfloat16 [512, 16384], P(None, 'head'), as said below
- up_value: bfloat16 [512, 16384], P(None, 'head'), may hold values from -0.25 to 0.25
Outputs:
- grad_queries: float32 [256, 16384], P('ctx', 'head')
- grad_latent: float32 [16384, 512], P(('ctx', 'head'))
- grad_up_key: float32 [512, 16384], P('ctx', 'head')
- grad_up_value: float32 [512, 16384], P('ctx', 'head')
Inputs may be any that keep to these rules, and one draw needn't show every extreme that they name: `queries`: entries lie within 64 in magnitude. `up_key`: entries lie within 4 / sqrt(512) in magnitude.
All inputs are finite; a program needn't handle non-finite values.
Results may differ from a plain program's by a relative error of at most 0.005.
Values may be sent and summed in bfloat16 or wider, within the bound.
A program may use at most 128 MiB of HBM per device.

v0:
```python
import math
import jax
import jax.numpy as jnp
from jax import lax
from jax.sharding import PartitionSpec as P

HD = 128


def joined(part, axis, combine):
    gathered = jax.tree.map(lambda a: lax.all_gather(a, axis), part)

    def take(source):
        return jax.tree.map(lambda a: lax.dynamic_index_in_dim(a, source, 0, False), gathered)

    return lax.fori_loop(
        1, lax.axis_size(axis), lambda source, state: combine(state, take(source)), take(0)
    )


def join_pairs(former, latter):
    maxima = jnp.maximum(former[0], latter[0])
    left_factor = jnp.exp(former[0] - maxima)
    right_factor = jnp.exp(latter[0] - maxima)
    return (maxima, former[1] * left_factor + latter[1] * right_factor)


def local(queries, grad_out, latent, up_key, up_value):
    scale = 1.0 / math.sqrt(HD)
    local_heads = queries.shape[1] // HD
    width = queries.shape[1]
    query_count = queries.shape[0]
    contract_cols = (((1,), (1,)), ((), ()))
    contract_rows = (((0,), (0,)), ((), ()))
    block = lax.all_gather(latent, "head", axis=0, tiled=True)
    key_rows = block.shape[0]
    total_len = key_rows * lax.axis_size("ctx")
    first_key = lax.axis_index("ctx") * key_rows
    key_block = jnp.dot(block, up_key, preferred_element_type=jnp.float32)
    value_block = jnp.dot(block, up_value, preferred_element_type=jnp.float32).astype(jnp.bfloat16)
    query_pos = total_len - query_count + lax.iota(jnp.int32, query_count)
    key_pos = first_key + lax.iota(jnp.int32, key_rows)
    visible = key_pos[None, :] <= query_pos[:, None]
    head_ids = jnp.arange(local_heads, dtype=jnp.int32)

    def head_inputs(head_index):
        offset = head_index * HD
        return (
            lax.dynamic_slice_in_dim(queries, offset, HD, 1),
            lax.dynamic_slice_in_dim(grad_out, offset, HD, 1),
            lax.dynamic_slice_in_dim(key_block, offset, HD, 1),
            lax.dynamic_slice_in_dim(value_block, offset, HD, 1),
        )

    def masked_scores(query_head, key_head):
        raw = (
            lax.dot_general(
                query_head.astype(jnp.float32),
                key_head,
                contract_cols,
                precision=lax.Precision.HIGHEST,
            )
            * scale
        )
        return jnp.where(visible, raw, -jnp.inf)

    def product_scores(grad_head, value_head):
        return lax.dot_general(
            grad_head, value_head, contract_cols, preferred_element_type=jnp.float32
        )

    def pick_row(table, head_index):
        return lax.dynamic_index_in_dim(table, head_index, 0, keepdims=False)

    def local_pair(head_index):
        query_head, grad_head, key_head, value_head = head_inputs(head_index)
        scores = masked_scores(query_head, key_head)
        maxima = jnp.max(scores, axis=1)
        return (maxima, jnp.sum(jnp.exp(scores - maxima[:, None]), axis=1))

    local_max, local_sum = lax.map(local_pair, head_ids)
    maxima, totals = joined((local_max, local_sum), "ctx", join_pairs)

    def local_delta(head_index):
        query_head, grad_head, key_head, value_head = head_inputs(head_index)
        scores = masked_scores(query_head, key_head)
        probs = (
            jnp.exp(scores - pick_row(maxima, head_index)[:, None])
            / pick_row(totals, head_index)[:, None]
        )
        return jnp.sum(probs * product_scores(grad_head, value_head), axis=1)

    deltas = lax.psum(lax.map(local_delta, head_ids), "ctx")

    def accumulate(head_index, carry):
        query_acc, grad_kv = carry
        query_head, grad_head, key_head, value_head = head_inputs(head_index)
        scores = masked_scores(query_head, key_head)
        probs = (
            jnp.exp(scores - pick_row(maxima, head_index)[:, None])
            / pick_row(totals, head_index)[:, None]
        )
        grad_probs = product_scores(grad_head, value_head)
        grad_scores = (probs * (grad_probs - pick_row(deltas, head_index)[:, None]) * scale).astype(
            jnp.bfloat16
        )
        query_part = jnp.dot(
            grad_scores.astype(jnp.float32), key_head, precision=lax.Precision.HIGHEST
        )
        key_grad = lax.dot_general(
            grad_scores, query_head, contract_rows, preferred_element_type=jnp.float32
        ).astype(jnp.bfloat16)
        value_grad = lax.dot_general(
            probs.astype(jnp.bfloat16), grad_head, contract_rows, preferred_element_type=jnp.float32
        ).astype(jnp.bfloat16)
        offset = head_index * HD
        anchor = jnp.zeros((), jnp.int32)
        query_acc = lax.dynamic_update_slice(query_acc, query_part, (anchor, offset))
        grad_kv = lax.dynamic_update_slice(grad_kv, key_grad, (anchor, offset))
        grad_kv = lax.dynamic_update_slice(grad_kv, value_grad, (anchor, width + offset))
        return (query_acc, grad_kv)

    start_state = (
        jnp.zeros((query_count, width), jnp.float32),
        jnp.zeros((key_rows, 2 * width), jnp.bfloat16),
    )
    query_acc, grad_kv = lax.fori_loop(0, local_heads, accumulate, start_state)
    up_both = jnp.concatenate([up_key, up_value], axis=1)
    grad_queries = lax.psum_scatter(query_acc, "ctx", scatter_dimension=0, tiled=True)
    weight_sums = lax.psum_scatter(
        lax.dot_general(block, grad_kv, contract_rows, preferred_element_type=jnp.float32),
        "ctx",
        scatter_dimension=0,
        tiled=True,
    )
    own_rows = latent.shape[0]
    summed = lax.psum(
        lax.dot_general(grad_kv, up_both, contract_cols, preferred_element_type=jnp.float32), "head"
    )
    grad_latent = lax.dynamic_slice_in_dim(summed, lax.axis_index("head") * own_rows, own_rows, 0)
    return (grad_queries, grad_latent, weight_sums[:, :width], weight_sums[:, width:])


def solution(mesh):
    return jax.shard_map(
        local,
        mesh=mesh,
        in_specs=(
            P(None, "head"),
            P(None, "head"),
            P(("ctx", "head"), None),
            P(None, "head"),
            P(None, "head"),
        ),
        out_specs=(P("ctx", "head"), P(("ctx", "head"), None), P("ctx", "head"), P("ctx", "head")),
        check_vma=False,
    )
```

profile of v0, /device:TPU:0, one launch (start us, length us, event | category | flops | bytes accessed | tf_op | source)
XLA Modules:
  0.0 633.1 jit_solution(3696228629027708976)
XLA Ops:
  8.0 53.2 %all-gather.4.cloned.1.call-done = bf16[2048,512]{1,0:T(8,128)(2,1)} async-done(((bf16[128,512]{1,0:T(8,128)(2,1)}), bf16[2048,512]{1,0:T(8,128)(2,1)}) %all-gather.4.cloned.1.call-update) | async-done | bytes 2097168 | tf_op jit(solution)/shard_map/all_gather | solution.py:35
  61.2 7.4 %fusion.52 = f32[2048,1024]{1,0:T(8,128)} fusion(bf16[2048,512]{1,0:T(8,128)(2,1)} %all-gather.4.cloned.1.call-done, bf16[512,1024]{1,0:T(8,128)(2,1)} %param.16), kind=kOutput, calls=%fused_computation.71 | convolution fusion | flops 2147483648 | bytes 11534336 | tf_op jit(solution)/shard_map/dot_general | solution.py:39
  68.6 34.9 %while.60 = (s32[]{:T(128)}, f32[8,256]{1,0:T(8,128)S(1)}, f32[8,256]{1,0:T(8,128)S(1)}, s32[8]{0:T(128)S(1)}, bf16[256,1024]{1,0:T(8,128)(2,1)S(1)}, /*index=5*...) while((s32[]{:T(128)}, f32[8,256]{1,0:T(8,128)S(1)}, ...), condition=%wide.region_3.4_spmd.clone, body=%wide.region_0.3_spmd.clone.sunk | while | flops 808451584 | bytes 5326015 | solution.py:81
  103.6 28.2 %all-gather.1 = f32[64,256]{1,0:T(8,128)S(1)} all-gather(f32[8,256]{1,0:T(8,128)S(1)} %get-tuple-element.493), channel_id=3, replica_groups=mesh['ctx'=8,'head'=16] {'ctx'}, dimensions={0}, use_global_device_ids=true | all-gather | bytes 73728 | tf_op jit(solution)/shard_map/all_gather | solution.py:11
  131.8 28.2 %all-gather = f32[64,256]{1,0:T(8,128)S(1)} all-gather(f32[8,256]{1,0:T(8,128)S(1)} %get-tuple-element.492), channel_id=2, replica_groups=mesh['ctx'=8,'head'=16] {'ctx'}, dimensions={0}, use_global_device_ids=true | all-gather | bytes 73728 | tf_op jit(solution)/shard_map/all_gather | solution.py:11
  160.2 5.9 convolution_convert_fusion.2
  166.1 60.3 %while.61 = (s32[]{:T(128)}, f32[8,256]{1,0:T(8,128)S(1)}, s32[8]{0:T(128)S(1)}, bf16[256,1024]{1,0:T(8,128)(2,1)S(1)}, f32[2048,1024]{1,0:T(8,128)}, /*index=5*...) while((s32[]{:T(128)}, f32[8,256]{1,0:T(8,128)S(1)}, ...), condition=%wide.region_8.9_spmd.clone, body=%wide.region_6.8_spmd.clone.sunk | while | flops 943193856 | bytes 5918977 | solution.py:93
  169.3 2.7 fusion.90
  176.9 2.7 fusion.90
  184.4 2.7 fusion.90
  191.9 2.7 fusion.90
  199.5 2.7 fusion.90
  207.0 2.7 fusion.90
  214.6 2.7 fusion.90
  222.1 2.7 fusion.90
  226.5 19.1 %psum.14 = f32[8,256]{1,0:T(8,128)S(1)} all-reduce(f32[8,256]{1,0:T(8,128)S(1)} %get-tuple-element.496), channel_id=1, replica_groups=mesh['ctx'=8,'head'=16] {'ctx'}, use_global_device_ids=true, to_apply=%region_9.10 | all-reduce | flops 2048 | bytes 16384 | tf_op jit(solution)/shard_map/psum | solution.py:93
  245.7 4.3 broadcast_in_dim.48
  250.0 80.9 %while.62 = (s32[]{:T(128)}, f32[256,1024]{1,0:T(8,128)S(1)}, bf16[2048,2048]{1,0:T(8,128)(2,1)}, bf16[256,1024]{1,0:T(8,128)(2,1)S(1)}, f32[2048,1024]{1,0:T(8,...) while((s32[]{:T(128)}, f32[256,1024]{1,0:T(8,128)S(1)}, ...), condition=%wide.region_11.12_spmd.clone, body=%wide.region_10.11_spmd.clone.sunk | while | flops 2019033088 | bytes 13522222 | solution.py:127
  250.0 2.8 fusion.102
  260.2 2.7 fusion.102
  270.3 2.7 fusion.102
  280.4 2.7 fusion.102
  290.5 2.7 fusion.102
  300.6 2.7 fusion.102
  310.7 2.7 fusion.102
  320.8 2.7 fusion.102
  330.9 10.5 %fusion.45 = f32[2048,512]{1,0:T(8,128)} fusion(bf16[2048,2048]{1,0:T(8,128)(2,1)} %get-tuple-element.498, bf16[512,1024]{1,0:T(8,128)(2,1)} %param.17, bf16[512,1024]{1,0:T(8,128)(2,1)S(1)} %copy-done.3), kind=kOutput, calls=%fused_computation.61 | convolution fusion | flops 4299161600 | bytes 14680064 | tf_op jit(solution)/shard_map/dot_general | solution.py:138
  343.0 9.8 %convolution_bitcast_fusion = f32[512,2048]{0,1:T(8,128)} fusion(bf16[2048,2048]{1,0:T(8,128)(2,1)} %get-tuple-element.498, bf16[2048,512]{1,0:T(8,128)(2,1)S(1)} %copy-done.2), kind=kOutput, calls=%fused_computation.60 | convolution fusion | flops 4294967296 | bytes 14680064 | tf_op jit(solution)/shard_map/dot_general | solution.py:131
  352.8 5.5 copy.13
  358.8 130.5 %all-reduce.2.cloned.1.call-done = f32[2048,512]{1,0:T(8,128)} async-done(((f32[2048,512]{1,0:T(8,128)}), f32[2048,512]{1,0:T(8,128)}) %all-reduce.2.cloned.1.call-update) | async-done | bytes 4194320 | tf_op jit(solution)/shard_map/psum | solution.py:137
  491.1 91.7 %reduce-scatter.7.cloned.1.call-done = f32[64,2048]{1,0:T(8,128)} async-done(((f32[512,2048]{1,0:T(8,128)}), f32[64,2048]{1,0:T(8,128)}) %reduce-scatter.7.cloned.1.call-update) | async-done | bytes 524304
  584.6 41.9 %reduce-scatter.5.cloned.1.call-done = f32[32,1024]{1,0:T(8,128)} async-done(((f32[256,1024]{1,0:T(8,128)}), f32[32,1024]{1,0:T(8,128)}) %reduce-scatter.5.cloned.1.call-update) | async-done | bytes 131088 | tf_op jit(solution)/shard_map/reduce_scatter | solution.py:129
  (158 shorter events, 113.6 us)
Async XLA Ops:
  7.2 54.0 %all-gather.4.cloned.1.call-start = ((), (), s32[]{:S(2)}) async-start(), calls=%async_computation.2 | async-start | bytes 2228224 | tf_op jit(solution)/shard_map/all_gather | solution.py:35
  7.9 481.5 %all-reduce.2.cloned.1.call-start = ((), (), s32[]{:S(2)}) async-start(), calls=%async_computation.4 | async-start | bytes 8388608 | tf_op jit(solution)/shard_map/psum | solution.py:137
  8.0 60.7 %copy-start.1 = (bf16[256,1024]{1,0:T(8,128)(2,1)S(1)}, bf16[256,1024]{1,0:T(8,128)(2,1)}, u32[]{:S(2)}) copy-start(bf16[256,1024]{1,0:T(8,128)(2,1)} %param.13) | copy-start | bytes 1572868
  68.6 91.6 %copy-start.4 = (bf16[512,1024]{1,0:T(8,128)(2,1)S(1)}, bf16[512,1024]{1,0:T(8,128)(2,1)}, u32[]{:S(2)}) copy-start(bf16[512,1024]{1,0:T(8,128)(2,1)} %param.17) | copy-start | bytes 3145732
  250.0 80.9 %copy-start.3 = (bf16[512,1024]{1,0:T(8,128)(2,1)S(1)}, bf16[512,1024]{1,0:T(8,128)(2,1)}, u32[]{:S(2)}) copy-start(bf16[512,1024]{1,0:T(8,128)(2,1)} %param.16) | copy-start | bytes 3145732
  330.9 10.5 %copy-start = (f32[256,1024]{1,0:T(8,128)}, f32[256,1024]{1,0:T(8,128)S(1)}, u32[]{:S(2)}) copy-start(f32[256,1024]{1,0:T(8,128)S(1)} %get-tuple-element.497) | copy-start | bytes 3145732
  341.4 1.6 copy-start.2
  341.4 241.3 %reduce-scatter.7.cloned.1.call-start = ((), (), s32[]{:S(2)}) async-start(), calls=%async_computation.5 | async-start | bytes 4718592
  358.3 268.3 %reduce-scatter.5.cloned.1.call-start = ((), (), s32[]{:S(2)}) async-start(), calls=%async_computation.3 | async-start | bytes 1179648 | tf_op jit(solution)/shard_map/reduce_scatter | solution.py:129
Sparse Core Ops, SparseCore 0:
  10.4 50.7 all-gather.3
  341.6 147.7 all-reduce.1
  491.8 90.8 reduce-scatter.6
  585.5 40.9 reduce-scatter.4
where the time goes:
time: 636 us; the launch traced here: 633 us
  waiting for transfers between devices  319 us (50%)
  matrix products  169 us (27%)
  blocking collectives  75.5 us (12%)
  loops' own time  26.6 us (4%)
  local copies, waits for them, and re-layouts  25.9 us (4%)
  between operations  13.9 us (2%)
    psum x1, waiting for transfers between devices, local(): lax.psum(lax.dot_general(grad_kv, up_both, contract_cols, preferred_eleme...  131 us
    unnamed x5, waiting for transfers between devices  92.9 us
    dot_general x24, matrix products, masked_scores(): lax.dot_general(query_head.astype(jnp.float32), key_head, contract_cols,...  63.4 us
    all_gather x2, blocking collectives, joined(): gathered = jax.tree.map(lambda a: lax.all_gather(a, axis), part)  56.4 us
    all_gather x1, waiting for transfers between devices, local(): block = lax.all_gather(latent, 'head', axis=0, tiled=True)  53.2 us
    reduce_scatter x1, waiting for transfers between devices, local(): lax.psum_scatter(query_acc, 'ctx', scatter_dimension=0, tiled=True)  41.9 us
    dot_general x16, matrix products, product_scores(): lax.dot_general(grad_head, value_head, contract_cols, preferred_element_t...  25.1 us
    another operation x1, loops' own time, local(): deltas = lax.psum(lax.map(local_delta, head_ids), 'ctx')  21 us
  transfers between devices with their start and end apart: 4, of which 4 were waited for; matrix products, arithmetic and copies ran while one was open for 3% of the time, Pallas kernels for 0%

commit v1 on v0

--- a/solution.py
+++ b/solution.py
@@ -134,8 +134,12 @@
         tiled=True,
     )
     own_rows = latent.shape[0]
-    summed = lax.psum(
-        lax.dot_general(grad_kv, up_both, contract_cols, preferred_element_type=jnp.float32), "head"
+    summed = jnp.sum(
+        lax.all_gather(
+            lax.dot_general(grad_kv, up_both, contract_cols, preferred_element_type=jnp.float32),
+            "head",
+        ),
+        axis=0,
     )
     grad_latent = lax.dynamic_slice_in_dim(summed, lax.axis_index("head") * own_rows, own_rows, 0)
     return (grad_queries, grad_latent, weight_sums[:, :width], weight_sums[:, width:])

time: 636 us -> 830 us (1.31)
  waiting for transfers between devices: 319 us -> 489 us
  other arithmetic: 3.64 us -> 26.9 us
    all_gather x0 -> x1, waiting for transfers between devices: none -> 344 us  [local(): lax.all_gather(lax.dot_general(grad_kv, up_both, contract_cols, preferred...]
    psum x1 -> x0, waiting for transfers between devices: 131 us -> none  [local(): lax.psum(lax.dot_general(grad_kv, up_both, contract_cols, preferred_eleme...]
    reduce_scatter x1, waiting for transfers between devices: 41.9 us -> 14.8 us  [local(): lax.psum_scatter(query_acc, 'ctx', scatter_dimension=0, tiled=True)]
    reduce_sum x0 -> x1, other arithmetic: none -> 23.3 us  [local(): jnp.sum(lax.all_gather(lax.dot_general(grad_kv, up_both, contract_cols, p...]
    unnamed x5, waiting for transfers between devices: 92.9 us -> 77.4 us
  transfers between devices with their start and end apart: 4 -> 4, of which waited for: 4 -> 4; matrix products, arithmetic and copies ran while one was open for 3% -> 4% of each run, Pallas kernels for 0% -> 0%
where the time goes in v1:
time: 830 us; the launch traced here: 827 us
  waiting for transfers between devices  489 us (59%)
  matrix products  169 us (20%)
  blocking collectives  75.5 us (9%)
  loops' own time  27.1 us (3%)
  other arithmetic  26.9 us (3%)
  local copies, waits for them, and re-layouts  25.6 us (3%)
  between operations  13.9 us (2%)
    all_gather x1, waiting for transfers between devices, local(): lax.all_gather(lax.dot_general(grad_kv, up_both, contract_cols, preferred...  344 us
    unnamed x5, waiting for transfers between devices  77.4 us
    dot_general x24, matrix products, masked_scores(): lax.dot_general(query_head.astype(jnp.float32), key_head, contract_cols,...  63.3 us
    all_gather x2, blocking collectives, joined(): gathered = jax.tree.map(lambda a: lax.all_gather(a, axis), part)  56.4 us
    all_gather x1, waiting for transfers between devices, local(): block = lax.all_gather(latent, 'head', axis=0, tiled=True)  53.2 us
    dot_general x16, matrix products, product_scores(): lax.dot_general(grad_head, value_head, contract_cols, preferred_element_t...  25.1 us
    reduce_sum x1, other arithmetic, local(): jnp.sum(lax.all_gather(lax.dot_general(grad_kv, up_both, contract_cols, p...  23.3 us
    another operation x1, loops' own time, local(): deltas = lax.psum(lax.map(local_delta, head_ids), 'ctx')  21 us
  transfers between devices with their start and end apart: 4, of which 4 were waited for; matrix products, arithmetic and copies ran while one was open for 4% of the time, Pallas kernels for 0%

profile of v1, /device:TPU:0, one launch (start us, length us, event | category | flops | bytes accessed | tf_op | source)
XLA Modules:
  0.0 827.1 jit_solution(1151273844812888880)
XLA Ops:
  8.0 53.2 %all-gather.6.cloned.1.call-done = bf16[2048,512]{1,0:T(8,128)(2,1)} async-done(((bf16[128,512]{1,0:T(8,128)(2,1)}), bf16[2048,512]{1,0:T(8,128)(2,1)}) %all-gather.6.cloned.1.call-update) | async-done | bytes 2097168 | tf_op jit(solution)/shard_map/all_gather | solution.py:35
  61.2 7.4 fusion.52
  68.6 35.4 %while.60 = (s32[]{:T(128)}, f32[8,256]{1,0:T(8,128)S(1)}, f32[8,256]{1,0:T(8,128)S(1)}, s32[8]{0:T(128)S(1)}, bf16[256,1024]{1,0:T(8,128)(2,1)S(1)}, /*index=5*...) while((s32[]{:T(128)}, f32[8,256]{1,0:T(8,128)S(1)}, ...), condition=%wide.region_3.4_spmd.clone, body=%wide.region_0.3_spmd.clone.sunk | while | flops 808451584 | bytes 5326015 | solution.py:81
  104.1 28.2 %all-gather.1 = f32[64,256]{1,0:T(8,128)S(1)} all-gather(f32[8,256]{1,0:T(8,128)S(1)} %get-tuple-element.493), channel_id=3, replica_groups=mesh['ctx'=8,'head'=16] {'ctx'}, dimensions={0}, use_global_device_ids=true | all-gather | bytes 73728 | tf_op jit(solution)/shard_map/all_gather | solution.py:11
  132.3 28.2 %all-gather = f32[64,256]{1,0:T(8,128)S(1)} all-gather(f32[8,256]{1,0:T(8,128)S(1)} %get-tuple-element.492), channel_id=2, replica_groups=mesh['ctx'=8,'head'=16] {'ctx'}, dimensions={0}, use_global_device_ids=true | all-gather | bytes 73728 | tf_op jit(solution)/shard_map/all_gather | solution.py:11
  160.8 5.9 convolution_convert_fusion.2
  166.7 60.3 %while.61 = (s32[]{:T(128)}, f32[8,256]{1,0:T(8,128)S(1)}, s32[8]{0:T(128)S(1)}, bf16[256,1024]{1,0:T(8,128)(2,1)S(1)}, f32[2048,1024]{1,0:T(8,128)}, /*index=5*...) while((s32[]{:T(128)}, f32[8,256]{1,0:T(8,128)S(1)}, ...), condition=%wide.region_8.9_spmd.clone, body=%wide.region_6.8_spmd.clone.sunk | while | flops 943193856 | bytes 5918977 | solution.py:93
  169.8 2.7 fusion.90
  177.4 2.7 fusion.90
  184.9 2.7 fusion.90
  192.5 2.7 fusion.90
  200.0 2.7 fusion.90
  215.1 2.7 fusion.90
  222.6 2.7 fusion.90
  227.0 19.1 %psum.7 = f32[8,256]{1,0:T(8,128)S(1)} all-reduce(f32[8,256]{1,0:T(8,128)S(1)} %get-tuple-element.496), channel_id=1, replica_groups=mesh['ctx'=8,'head'=16] {'ctx'}, use_global_device_ids=true, to_apply=%region_9.10 | all-reduce | flops 2048 | bytes 16384 | tf_op jit(solution)/shard_map/psum | solution.py:93
  246.2 4.3 broadcast_in_dim.48
  250.5 80.8 %while.62 = (s32[]{:T(128)}, f32[256,1024]{1,0:T(8,128)S(1)}, bf16[2048,2048]{1,0:T(8,128)(2,1)}, bf16[256,1024]{1,0:T(8,128)(2,1)S(1)}, f32[2048,1024]{1,0:T(8,...) while((s32[]{:T(128)}, f32[256,1024]{1,0:T(8,128)S(1)}, ...), condition=%wide.region_11.12_spmd.clone, body=%wide.region_10.11_spmd.clone.sunk | while | flops 2019033088 | bytes 13522222 | solution.py:127
  250.5 2.7 fusion.102
  260.6 2.7 fusion.102
  270.7 2.7 fusion.102
  280.8 2.7 fusion.102
  290.9 2.7 fusion.102
  301.0 2.7 fusion.102
  311.1 2.7 fusion.102
  321.2 2.7 fusion.102
  331.3 10.8 %convolution_bitcast_fusion = f32[512,2048]{0,1:T(8,128)} fusion(bf16[2048,2048]{1,0:T(8,128)(2,1)} %get-tuple-element.498, bf16[2048,512]{1,0:T(8,128)(2,1)} %all-gather.6.cloned.1.call-done), kind=kOutput, calls=%fused_computation.60 | convolution fusion | flops 4294967296 | bytes 14680064 | tf_op jit(solution)/shard_map/dot_general | solution.py:131
  342.1 5.5 copy.13
  348.8 9.6 %fusion.45 = f32[2048,512]{1,0:T(8,128)} fusion(bf16[2048,2048]{1,0:T(8,128)(2,1)} %get-tuple-element.498, bf16[512,1024]{1,0:T(8,128)(2,1)S(1)} %copy-done.3, bf16[512,1024]{1,0:T(8,128)(2,1)S(1)} %copy-done.2), kind=kOutput, calls=%fused_computation.61 | convolution fusion | flops 4299161600 | bytes 14680064 | tf_op jit(solution)/shard_map/dot_general | solution.py:139
  359.1 76.2 %reduce-scatter.7.cloned.1.call-done = f32[64,2048]{1,0:T(8,128)} async-done(((f32[512,2048]{1,0:T(8,128)}), f32[64,2048]{1,0:T(8,128)}) %reduce-scatter.7.cloned.1.call-update) | async-done | bytes 524304
  437.1 343.7 %all-gather.8.cloned.1.call-done = f32[32768,512]{1,0:T(8,128)} async-done(((f32[2048,512]{1,0:T(8,128)}), f32[32768,512]{1,0:T(8,128)}) %all-gather.8.cloned.1.call-update) | async-done | bytes 67108880 | tf_op jit(solution)/shard_map/all_gather | solution.py:138
  780.8 23.3 %reduce_sum.27 = f32[2048,512]{1,0:T(8,128)} reduce(f32[16,2048,512]{2,1,0:T(8,128)} %bitcast.4, f32[]{:T(128)} %constant.194.clone.1), dimensions={0}, to_apply=%region_13.14 | reduce | flops 15728640 | bytes 71303168 | tf_op jit(solution)/shard_map/reduce_sum | solution.py:137
  805.8 14.8 %reduce-scatter.5.cloned.1.call-done = f32[32,1024]{1,0:T(8,128)} async-done(((f32[256,1024]{1,0:T(8,128)}), f32[32,1024]{1,0:T(8,128)}) %reduce-scatter.5.cloned.1.call-update) | async-done | bytes 131088 | tf_op jit(solution)/shard_map/reduce_scatter | solution.py:129
  (157 shorter events, 116.0 us)
Async XLA Ops:
  7.2 54.0 %all-gather.6.cloned.1.call-start = ((), (), s32[]{:S(2)}) async-start(), calls=%async_computation.2 | async-start | bytes 2228224 | tf_op jit(solution)/shard_map/all_gather | solution.py:35
  7.9 427.3 %reduce-scatter.7.cloned.1.call-start = ((), (), s32[]{:S(2)}) async-start(), calls=%async_computation.5 | async-start | bytes 4718592
  8.0 60.6 %copy-start.1 = (bf16[256,1024]{1,0:T(8,128)(2,1)S(1)}, bf16[256,1024]{1,0:T(8,128)(2,1)}, u32[]{:S(2)}) copy-start(bf16[256,1024]{1,0:T(8,128)(2,1)} %param.13) | copy-start | bytes 1572868
  68.6 92.1 %copy-start.3 = (bf16[512,1024]{1,0:T(8,128)(2,1)S(1)}, bf16[512,1024]{1,0:T(8,128)(2,1)}, u32[]{:S(2)}) copy-start(bf16[512,1024]{1,0:T(8,128)(2,1)} %param.17) | copy-start | bytes 3145732
  331.3 10.9 %copy-start = (f32[256,1024]{1,0:T(8,128)}, f32[256,1024]{1,0:T(8,128)S(1)}, u32[]{:S(2)}) copy-start(f32[256,1024]{1,0:T(8,128)S(1)} %get-tuple-element.497) | copy-start | bytes 3145732
  347.6 1.2 copy-start.2
  347.6 433.2 %all-gather.8.cloned.1.call-start = ((), (), s32[]{:S(2)}) async-start(), calls=%async_computation.4 | async-start | bytes 71303168 | tf_op jit(solution)/shard_map/all_gather | solution.py:138
  358.5 462.1 %reduce-scatter.5.cloned.1.call-start = ((), (), s32[]{:S(2)}) async-start(), calls=%async_computation.3 | async-start | bytes 1179648 | tf_op jit(solution)/shard_map/reduce_scatter | solution.py:129
Sparse Core Ops, SparseCore 0:
  10.4 50.7 all-gather.5
  347.8 87.4 reduce-scatter.6
  437.7 343.0 all-gather.7
  783.6 36.9 reduce-scatter.4
